TPU v7x, 256 devices: a whole 4x4x8 slice. The times are simulated.
256 devices in a mesh: graph: 32 (over z, y), feat: 8 (over x, core).
Axes of the slice: x: 4, y: 4, z: 8, core: 2. Of those that a mesh axis runs over, the one named last changes fastest.
Arguments:
- features: bfloat16 [65536, 1024], P('graph', 'feat'), may hold values from -6 to 6
- w_self: bfloat16 [1024, 1024], replicated, may hold values from -0.1875 to 0.1875
- w_neigh: bfloat16 [1024, 1024], replicated, may hold values from -0.1875 to 0.1875
- adjacency: bfloat16 [4096, 128, 128], P('graph'), may hold values from 0 to 1.5, as said below
- block_source: int32 [4096], P('graph'), may hold values from 0 to 15
- block_to_slot: int32 [4096], P('graph'), may hold values from 0 to 63
- send_rows: int32 [32, 32, 256], P('graph'), may hold values from 0 to 2047
- send_counts: int32 [32, 32], P('graph'), may hold values from 64 to 256, as said below
- degree: int32 [65536], P('graph'), may hold values from 8 to 32
- cotangent: bfloat16 [65536, 1024], P('graph', 'feat'), may hold values from -6 to 6
Outputs:
- hidden_out: bfloat16 [65536, 1024], P('graph', 'feat')
- grad_features: bfloat16 [65536, 1024], P('graph', 'feat')
- grad_self: float32 [1024, 1024], P('feat')
- grad_neigh: float32 [1024, 1024], P('feat')
Inputs may be any that keep to these rules, and one draw needn't show every extreme that they name: Slots 0 to send_counts[p, q] - 1 from p to q are live; in every draw some partition receives 256 live slots from every partition. `adjacency`: edge weights; a block is mostly zeros.
All inputs are finite; a program needn't handle non-finite values.
Results may differ from a plain program's by a relative error of at most 0.0066.
Values may be sent and summed in bfloat16 or wider, within the bound.
No kernel may reach another device: no remote copies, remote signals or barrier semaphores. Data moves between devices by JAX's collectives and lax.ppermute only.
A program may use at most 128 MiB of HBM per device.

v0:
```python
import jax
import jax.numpy as jnp
from jax import lax
from jax.sharding import PartitionSpec as P


def silu_slope(values):
    sig = jax.nn.sigmoid(values)
    return sig * (1.0 + values * (1.0 - sig))


def on_device(
    features,
    w_self,
    w_neigh,
    adjacency,
    block_source,
    block_to_slot,
    send_rows,
    send_counts,
    degree,
    cotangent,
):
    node_rows, feat_cols = features.shape
    part_count = lax.axis_size("graph")
    block_size = adjacency.shape[1]
    slot_cap = send_rows.shape[2]
    slot_total = part_count * slot_cap // block_size
    source_count = node_rows // block_size
    column_start = lax.axis_index("feat") * feat_cols
    sources = features.reshape(source_count, block_size, feat_cols)
    picked = jnp.take(sources, block_source, axis=0)
    prods = jnp.einsum("kij,kjd->kid", adjacency, picked, preferred_element_type=jnp.float32)
    slot_sums = jax.ops.segment_sum(prods, block_to_slot, num_segments=slot_total)
    live_counts = send_counts[0]
    is_live = jnp.arange(slot_cap, dtype=jnp.int32)[None, :] < live_counts[:, None]
    outgoing = jnp.where(
        is_live[:, :, None], slot_sums.reshape(part_count, slot_cap, feat_cols), 0.0
    ).astype(jnp.bfloat16)
    row_ids = jnp.where(is_live, send_rows[0], -1)
    incoming, incoming_ids = (
        lax.all_to_all(outgoing, "graph", split_axis=0, concat_axis=0, tiled=True),
        lax.all_to_all(row_ids, "graph", split_axis=0, concat_axis=0, tiled=True),
    )
    valid_slot = incoming_ids >= 0
    target_rows = jnp.where(valid_slot, incoming_ids, node_rows).reshape(-1)
    neighbor_sum = (
        jnp.zeros((node_rows, feat_cols), jnp.float32)
        .at[target_rows]
        .add(incoming.reshape(-1, feat_cols).astype(jnp.float32), mode="drop")
    )
    degrees = degree.astype(jnp.float32)[:, None]
    neighbor_mean = (neighbor_sum / degrees).astype(jnp.bfloat16)
    self_rows = lax.dynamic_slice_in_dim(w_self, column_start, feat_cols, 0)
    neigh_rows = lax.dynamic_slice_in_dim(w_neigh, column_start, feat_cols, 0)
    own_term = lax.dot_general(
        self_rows, features, (((0,), (1,)), ((), ())), preferred_element_type=jnp.float32
    )
    agg_term = lax.dot_general(
        neigh_rows, neighbor_mean, (((0,), (1,)), ((), ())), preferred_element_type=jnp.float32
    )
    pre_act = lax.psum_scatter(own_term + agg_term, "feat", scatter_dimension=0, tiled=True).T
    hidden_out = jax.nn.silu(pre_act).astype(jnp.bfloat16)
    grad_pre = (cotangent.astype(jnp.float32) * silu_slope(pre_act)).astype(jnp.bfloat16)
    grad_full = lax.all_gather(grad_pre, "feat", axis=1, tiled=True)
    local_self = lax.dot_general(
        features, grad_full, (((0,), (0,)), ((), ())), preferred_element_type=jnp.float32
    )
    local_neigh = lax.dot_general(
        neighbor_mean, grad_full, (((0,), (0,)), ((), ())), preferred_element_type=jnp.float32
    )
    grad_self, grad_neigh = lax.psum((local_self, local_neigh), "graph")
    self_grad = lax.dot_general(
        grad_full, self_rows, (((1,), (1,)), ((), ())), preferred_element_type=jnp.float32
    )
    back_rows = (
        lax.dot_general(
            grad_full, neigh_rows, (((1,), (1,)), ((), ())), preferred_element_type=jnp.float32
        )
        / degrees
    ).astype(jnp.bfloat16)
    lookup = jnp.where(valid_slot, incoming_ids, 0)
    sending_back = jnp.where(valid_slot[:, :, None], jnp.take(back_rows, lookup, axis=0), 0.0)
    returned = lax.all_to_all(sending_back, "graph", split_axis=0, concat_axis=0, tiled=True)
    slot_blocks = returned.reshape(slot_total, block_size, feat_cols)
    chosen = jnp.take(slot_blocks, block_to_slot, axis=0)
    contrib = jnp.einsum("kij,kid->kjd", adjacency, chosen, preferred_element_type=jnp.float32)
    neigh_grad = jax.ops.segment_sum(contrib, block_source, num_segments=source_count).reshape(
        node_rows, feat_cols
    )
    grad_features = (self_grad + neigh_grad).astype(jnp.bfloat16)
    return (hidden_out, grad_features, grad_self, grad_neigh)


def solution(mesh):
    placed = (
        P("graph", "feat"),
        P(),
        P(),
        P("graph", None, None),
        P("graph"),
        P("graph"),
        P("graph", None, None),
        P("graph", None),
        P("graph"),
        P("graph", "feat"),
    )
    return jax.shard_map(
        on_device,
        mesh=mesh,
        in_specs=placed,
        out_specs=(P("graph", "feat"), P("graph", "feat"), P("feat", None), P("feat", None)),
        check_vma=False,
    )
```

profile of v0, /device:TPU:2, one launch (start us, length us, event | category | flops | bytes accessed | tf_op | source)
XLA Modules:
  0.0 545.4 jit_solution(14531779473950020415)
XLA Ops:
  7.2 0.0 copy-start
  7.2 1.6 compare_select_fusion.4
  8.8 11.5 %all-to-all-start = ((s32[32,1,256]{2,1,0:T(1,128)}), s32[32,1,256]{2,1,0:T(1,128)S(1)}, u32[]{:S(2)}, u32[]{:S(2)}) async-start(s32[32,1,256]{2,1,0:T(1,128)} %compare_select_fusion.4), calls=%async_computation | async-start | bytes 65536 | tf_op jit(solution)/shard_map/all_to_all | solution.py:43
  20.3 0.7 compare_and_fusion.2
  21.0 0.7 compare_select_fusion.7
  21.6 0.7 iota_compare_fusion
  22.4 4.1 gather_fusion
  26.4 9.9 %fusion.9 = f32[128,128,128]{1,2,0:T(8,128)} fusion(bf16[128,128,128]{2,1,0:T(8,128)(2,1)} %param.13, bf16[128,128,128]{2,1,0:T(8,128)(2,1)} %gather_fusion, pred[128]{0:T(512)(128)(4,1)S(1)} %compare_and_fusion.2), kind=kOutput, calls=%fused_computation.17 | convolution fusion | flops 538968064 | bytes 16777344 | tf_op jit(solution)/shard_map/kij,kjd->kid/dot_general | solution.py:33
  36.4 9.0 %copy.27 = f32[128,128,128]{2,1,0:T(8,128)} copy(f32[128,128,128]{1,2,0:T(8,128)} %fusion.9) | data formatting | bytes 16777216 | tf_op jit(solution)/shard_map/kij,kjd->kid/dot_general | solution.py:33
  45.4 2.5 broadcast_in_dim.92
  47.9 26.8 %scatter_fusion = f32[64,128,128]{2,1,0:T(8,128)} fusion(f32[64,128,128]{2,1,0:T(8,128)} %broadcast_in_dim.92, s32[128]{0:T(128)S(1)} %copy-done.8, f32[128,128,128]{2,1,0:T(8,128)} %copy.27), kind=kCustom, calls=%fused_computation.3 | custom fusion | flops 2097152 | bytes 25166336 | tf_op jit(solution)/shard_map/scatter-add | solution.py:34
  74.7 4.9 fusion.2
  79.6 0.0 all-to-all-done
  79.6 9.7 %all-to-all-start.1 = ((bf16[32,256,128]{2,1,0:T(8,128)(2,1)}), bf16[32,256,128]{2,1,0:T(8,128)(2,1)}, u32[]{:S(2)}, u32[]{:S(2)}) async-start(bf16[32,256,128]{2,1,0:T(8,128)(2,1)} %fusion.2), calls=%async_computation.1 | async-start | bytes 4194304 | tf_op jit(solution)/shard_map/all_to_all | solution.py:42
  89.3 0.0 reduce-scatter.2.cloned.1.call-start
  89.4 5.5 %fusion.31 = f32[1024,2048]{1,0:T(8,128)} fusion(bf16[2048,128]{1,0:T(8,128)(2,1)S(1)} %copy-done.2, bf16[1024,1024]{1,0:T(8,128)(2,1)} %param.11, s32[]{:T(128)S(6)} %select_n.95), kind=kOutput, calls=%fused_computation.43 | convolution fusion | flops 536870912 | bytes 9175044 | tf_op jit(solution)/shard_map/dot_general | solution.py:56
  94.8 0.1 compare_select_fusion.2
  94.9 44.0 %all-to-all-done.1 = bf16[32,256,128]{2,1,0:T(8,128)(2,1)} async-done(((bf16[32,256,128]{2,1,0:T(8,128)(2,1)}), bf16[32,256,128]{2,1,0:T(8,128)(2,1)}, u32[]{:S(2)}, u32[]{:S(2)}) %all-to-all-start.1) | async-done | bytes 2097184 | tf_op jit(solution)/shard_map/all_to_all | solution.py:42
  138.8 45.6 %scatter_custom_fusion.1 = f32[2048,128]{1,0:T(8,128)} fusion(s32[8192]{0:T(1024)S(1)} %bitcast.71, bf16[8192,128]{1,0:T(8,128)(2,1)} %bitcast.15, f32[]{:T(128)} %constant.32.clone.1), kind=kCustom, calls=%fused_computation.7 | custom fusion | flops 2097152 | bytes 3145732 | tf_op jit(solution)/shard_map/scatter-add | solution.py:50
  184.4 8.3 %convolution_add_fusion = f32[1024,2048]{1,0:T(8,128)} fusion(f32[1024,2048]{1,0:T(8,128)} %fusion.31, bf16[1024,1024]{1,0:T(8,128)(2,1)S(1)} %copy-done, s32[]{:T(128)S(6)} %select_n.95, f32[2048,128]{1,0:T(8,128)} %scatter_custom_fusion.1, f32[2048]{0:T(1024)S(1)} %convert_element_type.35), kind=kOutput, calls=%fused_computation.6 | convolution fusion | flops 539492352 | bytes 18096132 | tf_op jit(solution)/shard_map/dot_general | solution.py:59
  192.7 0.0 reduce-scatter.2.cloned.1.call-update
  192.8 0.2 all-gather.2.cloned.1.call-start
  193.0 1.2 copy.28
  194.2 48.7 %reduce-scatter.2.cloned.1.call-done = f32[128,2048]{1,0:T(8,128)} async-done(((f32[1024,2048]{1,0:T(8,128)}), f32[128,2048]{1,0:T(8,128)}) %reduce-scatter.2.cloned.1.call-update) | async-done | bytes 1048592 | tf_op jit(solution)/shard_map/reduce_scatter | solution.py:62
  242.9 2.6 fusion.26
  245.5 0.0 all-gather.2.cloned.1.call-update
  245.6 0.1 compare_select_fusion
  245.7 35.7 %all-gather.2.cloned.1.call-done = bf16[2048,1024]{0,1:T(8,128)(2,1)} async-done(((bf16[2048,128]{0,1:T(8,128)(2,1)}), bf16[2048,1024]{0,1:T(8,128)(2,1)}) %all-gather.2.cloned.1.call-update) | async-done | bytes 4194320 | tf_op jit(solution)/shard_map/all_gather | solution.py:65
  281.4 3.6 fusion.16
  285.0 24.0 %gather_fusion.1 = bf16[8192,128]{1,0:T(8,128)(2,1)S(1)} fusion(bf16[2048,128]{1,0:T(8,128)(2,1)S(1)} %fusion.16, s32[8192]{0:T(1024)S(1)} %broadcast_clamp_fusion), kind=kCustom, calls=%fused_computation.1 | custom fusion | bytes 4227072 | tf_op jit(solution)/shard_map/jit(_take)/gather | solution.py:83
  309.0 4.6 select_select_fusion
  313.7 9.9 %all-to-all-start.2 = ((bf16[32,256,128]{2,1,0:T(8,128)(2,1)}), bf16[32,256,128]{2,1,0:T(8,128)(2,1)S(1)}, u32[]{:S(2)}, u32[]{:S(2)}) async-start(bf16[32,256,128]{2,1,0:T(8,128)(2,1)} %select_select_fusion), calls=%async_computation.3 | async-start | bytes 4194304 | tf_op jit(solution)/shard_map/all_to_all | solution.py:84
  323.5 0.0 all-reduce.3.cloned.1.call-start
  323.6 4.4 convolution_bitcast_fusion
  328.0 2.8 fusion.39
  330.8 0.0 all-reduce.3.cloned.1.call-update
  330.9 1.0 copy.31
  331.9 162.1 %all-reduce.3.cloned.1.call-done = (f32[128,1024]{0,1:T(8,128)}, f32[128,1024]{1,0:T(8,128)}) async-done(((f32[128,1024]{0,1:T(8,128)}, f32[128,1024]{1,0:T(8,128)}), (f32[128,1024]{0,1:T(8,128)}, f32[128,1024]{1,0:T(8,128)})) %all-reduce.3.cloned.1.call-update) | async-done | bytes 1048592 | tf_op jit(solution)/shard_map/psum | solution.py:72
  494.0 2.0 copy.32
  496.0 0.0 all-to-all-done.2
  496.0 3.0 gather_fusion.2
  499.0 8.4 %fusion.12 = f32[128,128,128]{1,2,0:T(8,128)} fusion(bf16[128,128,128]{2,1,0:T(8,128)(2,1)} %param.13, bf16[128,128,128]{2,1,0:T(8,128)(2,1)} %gather_fusion.2, pred[128]{0:T(512)(128)(4,1)S(1)} %compare_and_fusion.1), kind=kOutput, calls=%fused_computation.18 | convolution fusion | flops 538968064 | bytes 16777344 | tf_op jit(solution)/shard_map/kij,kid->kjd/dot_general | solution.py:87
  507.4 9.0 %copy.30 = f32[128,128,128]{2,1,0:T(8,128)} copy(f32[128,128,128]{1,2,0:T(8,128)} %fusion.12) | data formatting | bytes 16777216 | tf_op jit(solution)/shard_map/kij,kid->kjd/dot_general | solution.py:87
  516.4 0.1 broadcast_in_dim.98
  516.5 17.0 %scatter_fusion.1 = f32[16,128,128]{2,1,0:T(8,128)S(1)} fusion(f32[16,128,128]{2,1,0:T(8,128)S(1)} %broadcast_in_dim.98, s32[128]{0:T(128)S(1)} %copy-done.9, f32[128,128,128]{2,1,0:T(8,128)} %copy.30), kind=kCustom, calls=%fused_computation.5 | custom fusion | flops 2097152 | bytes 25166336 | tf_op jit(solution)/shard_map/scatter-add | solution.py:88
  533.6 0.0 copy-start.1
  533.6 4.5 fusion.15
  538.0 0.8 copy.44
  (25 shorter events, 0.1 us)
Async XLA Ops:
  7.2 177.2 %copy-start = (bf16[1024,1024]{1,0:T(8,128)(2,1)S(1)}, bf16[1024,1024]{1,0:T(8,128)(2,1)}, u32[]{:S(2)}) copy-start(bf16[1024,1024]{1,0:T(8,128)(2,1)} %param.12) | copy-start | bytes 6291460
  8.8 70.8 %all-to-all-start = ((s32[32,1,256]{2,1,0:T(1,128)}), s32[32,1,256]{2,1,0:T(1,128)S(1)}, u32[]{:S(2)}, u32[]{:S(2)}) async-start(s32[32,1,256]{2,1,0:T(1,128)} %compare_select_fusion.4), calls=%async_computation | async-start | bytes 65536 | tf_op jit(solution)/shard_map/all_to_all | solution.py:43
  45.4 2.5 copy-start.8
  74.7 14.6 %copy-start.7 = (s32[2048]{0:T(1024)S(1)}, s32[2048]{0:T(1024)}, u32[]{:S(2)}) copy-start(s32[2048]{0:T(1024)} %param.18) | copy-start | bytes 24580
  74.7 14.6 %copy-start.2 = (bf16[2048,128]{1,0:T(8,128)(2,1)S(1)}, bf16[2048,128]{1,0:T(8,128)(2,1)}, u32[]{:S(2)}) copy-start(bf16[2048,128]{1,0:T(8,128)(2,1)} %param.10) | copy-start | bytes 1572868
  79.6 59.3 %all-to-all-start.1 = ((bf16[32,256,128]{2,1,0:T(8,128)(2,1)}), bf16[32,256,128]{2,1,0:T(8,128)(2,1)}, u32[]{:S(2)}, u32[]{:S(2)}) async-start(bf16[32,256,128]{2,1,0:T(8,128)(2,1)} %fusion.2), calls=%async_computation.1 | async-start | bytes 4194304 | tf_op jit(solution)/shard_map/all_to_all | solution.py:42
  89.3 153.6 %reduce-scatter.2.cloned.1.call-start = ((), (), s32[]{:S(2)}) async-start(), calls=%async_computation.4 | async-start | bytes 9437184 | tf_op jit(solution)/shard_map/reduce_scatter | solution.py:62
  192.8 88.6 %all-gather.2.cloned.1.call-start = ((), (), s32[]{:S(2)}) async-start(), calls=%async_computation.5 | async-start | bytes 4718592 | tf_op jit(solution)/shard_map/all_gather | solution.py:65
  313.7 182.3 %all-to-all-start.2 = ((bf16[32,256,128]{2,1,0:T(8,128)(2,1)}), bf16[32,256,128]{2,1,0:T(8,128)(2,1)S(1)}, u32[]{:S(2)}, u32[]{:S(2)}) async-start(bf16[32,256,128]{2,1,0:T(8,128)(2,1)} %select_select_fusion), calls=%async_computation.3 | async-start | bytes 4194304 | tf_op jit(solution)/shard_map/all_to_all | solution.py:84
  323.5 170.4 %all-reduce.3.cloned.1.call-start = ((), (), s32[]{:S(2)}) async-start(), calls=%async_computation.6 | async-start | bytes 2097152 | tf_op jit(solution)/shard_map/psum | solution.py:72
  323.6 4.4 copy-start.3
  323.6 4.4 copy-start.4
  328.0 2.9 copy-start.5
  507.4 9.1 %copy-start.9 = (s32[128]{0:T(128)S(1)}, s32[128]{0:T(128)}, u32[]{:S(2)}) copy-start(s32[128]{0:T(128)} %param.14) | copy-start | bytes 1540
  533.6 4.5 copy-start.6
  533.6 5.3 copy-start.1
Sparse Core Ops, SparseCore 0:
  192.9 49.9 reduce-scatter.1
  245.7 35.6 all-gather.1
  330.9 162.9 all-reduce.2
where the time goes:
time: 547 us; the launch traced here: 545 us
  waiting for transfers between devices  290 us (53%)
  other arithmetic  105 us (19%)
  local copies, waits for them, and re-layouts  56.8 us (10%)
  matrix products  47.4 us (9%)
  starting transfers between devices  31.3 us (6%)
  between operations  14 us (3%)
    psum x1, waiting for transfers between devices, on_device(): grad_self, grad_neigh = lax.psum((local_self, local_neigh), 'graph')  162 us
    reduce_scatter x1, waiting for transfers between devices, on_device(): lax.psum_scatter(own_term + agg_term, 'feat', scatter_dimension=0, tiled=...  48.7 us
    scatter-add x1, other arithmetic, on_device(): neighbor_sum = jnp.zeros((node_rows, feat_cols), jnp.float32).at[target_r...  45.6 us
    all_to_all x1, waiting for transfers between devices, on_device(): lax.all_to_all(outgoing, 'graph', split_axis=0, concat_axis=0, tiled=True)  44 us
    all_gather x1, waiting for transfers between devices, on_device(): grad_full = lax.all_gather(grad_pre, 'feat', axis=1, tiled=True)  35.7 us
    scatter-add x1, other arithmetic, on_device(): jax.ops.segment_sum(prods, block_to_slot, num_segments=slot_total)  26.8 us
    gather x1, local copies, waits for them, and re-layouts, on_device(): jnp.take(back_rows, lookup, axis=0)  24 us
    scatter-add x1, other arithmetic, on_device(): jax.ops.segment_sum(contrib, block_source, num_segments=source_count)  17 us
  transfers between devices with their start and end apart: 6, of which 4 were waited for; matrix products, arithmetic and copies ran while one was open for 14% of the time, Pallas kernels for 0%

commit v1 on v0

--- a/solution.py
+++ b/solution.py
@@ -62,7 +62,12 @@
     pre_act = lax.psum_scatter(own_term + agg_term, "feat", scatter_dimension=0, tiled=True).T
     hidden_out = jax.nn.silu(pre_act).astype(jnp.bfloat16)
     grad_pre = (cotangent.astype(jnp.float32) * silu_slope(pre_act)).astype(jnp.bfloat16)
-    grad_full = lax.all_gather(grad_pre, "feat", axis=1, tiled=True)
+    grad_full = jnp.concatenate(
+        lax.all_to_all(
+            jnp.stack(lax.axis_size("feat") * [grad_pre]), "feat", split_axis=0, concat_axis=0
+        ),
+        axis=1,
+    )
     local_self = lax.dot_general(
         features, grad_full, (((0,), (0,)), ((), ())), preferred_element_type=jnp.float32
     )

time: 547 us -> 569 us (1.040)
  waiting for transfers between devices: 290 us -> 301 us
  starting transfers between devices: 31.3 us -> 38.7 us
    all_to_all x0 -> x1, waiting for transfers between devices: none -> 48.2 us  [on_device(): lax.all_to_all(jnp.stack(lax.axis_size('feat') * [grad_pre]), 'feat', spl...]
    all_gather x1 -> x0, waiting for transfers between devices: 35.7 us -> none  [on_device(): grad_full = lax.all_gather(grad_pre, 'feat', axis=1, tiled=True)]
    all_to_all x0 -> x1, starting transfers between devices: none -> 7.37 us  [on_device(): lax.all_to_all(jnp.stack(lax.axis_size('feat') * [grad_pre]), 'feat', spl...]
where the time goes in v1:
time: 569 us; the launch traced here: 567 us
  waiting for transfers between devices  301 us (53%)
  other arithmetic  105 us (18%)
  local copies, waits for them, and re-layouts  59.3 us (10%)
  matrix products  49.5 us (9%)
  starting transfers between devices  38.7 us (7%)
  between operations  14.2 us (2%)
    psum x1, waiting for transfers between devices, on_device(): grad_self, grad_neigh = lax.psum((local_self, local_neigh), 'graph')  159 us
    reduce_scatter x1, waiting for transfers between devices, on_device(): lax.psum_scatter(own_term + agg_term, 'feat', scatter_dimension=0, tiled=...  48.9 us
    all_to_all x1, waiting for transfers between devices, on_device(): lax.all_to_all(jnp.stack(lax.axis_size('feat') * [grad_pre]), 'feat', spl...  48.2 us
    scatter-add x1, other arithmetic, on_device(): neighbor_sum = jnp.zeros((node_rows, feat_cols), jnp.float32).at[target_r...  45.6 us
    all_to_all x1, waiting for transfers between devices, on_device(): lax.all_to_all(outgoing, 'graph', split_axis=0, concat_axis=0, tiled=True)  44 us
    scatter-add x1, other arithmetic, on_device(): jax.ops.segment_sum(prods, block_to_slot, num_segments=slot_total)  26.7 us
    gather x1, local copies, waits for them, and re-layouts, on_device(): jnp.take(back_rows, lookup, axis=0)  24 us
    scatter-add x1, other arithmetic, on_device(): jax.ops.segment_sum(contrib, block_source, num_segments=source_count)  17 us
  transfers between devices with their start and end apart: 6, of which 4 were waited for; matrix products, arithmetic and copies ran while one was open for 14% of the time, Pallas kernels for 0%

profile of v1, /device:TPU:2, one launch (start us, length us, event | category | flops | bytes accessed | tf_op | source)
XLA Modules:
  0.0 567.5 jit_solution(11346938930478799305)
XLA Ops:
  7.2 0.0 copy-start
  7.2 1.6 compare_select_fusion.4
  8.8 11.5 %all-to-all-start = ((s32[32,1,256]{2,1,0:T(1,128)}), s32[32,1,256]{2,1,0:T(1,128)S(1)}, u32[]{:S(2)}, u32[]{:S(2)}) async-start(s32[32,1,256]{2,1,0:T(1,128)} %compare_select_fusion.4), calls=%async_computation | async-start | bytes 65536 | tf_op jit(solution)/shard_map/all_to_all | solution.py:43
  20.3 0.7 compare_and_fusion.2
  21.0 0.7 compare_select_fusion.7
  21.6 0.7 iota_compare_fusion
  22.4 4.1 gather_fusion
  26.4 9.9 %fusion.9 = f32[128,128,128]{1,2,0:T(8,128)} fusion(bf16[128,128,128]{2,1,0:T(8,128)(2,1)} %param.13, bf16[128,128,128]{2,1,0:T(8,128)(2,1)} %gather_fusion, pred[128]{0:T(512)(128)(4,1)S(1)} %compare_and_fusion.2), kind=kOutput, calls=%fused_computation.17 | convolution fusion | flops 538968064 | bytes 16777344 | tf_op jit(solution)/shard_map/kij,kjd->kid/dot_general | solution.py:33
  36.4 9.0 %copy.28 = f32[128,128,128]{2,1,0:T(8,128)} copy(f32[128,128,128]{1,2,0:T(8,128)} %fusion.9) | data formatting | bytes 16777216 | tf_op jit(solution)/shard_map/kij,kjd->kid/dot_general | solution.py:33
  45.4 2.5 broadcast_in_dim.92
  47.8 26.7 %scatter_fusion = f32[64,128,128]{2,1,0:T(8,128)} fusion(f32[64,128,128]{2,1,0:T(8,128)} %broadcast_in_dim.92, s32[128]{0:T(128)S(1)} %copy-done.7, f32[128,128,128]{2,1,0:T(8,128)} %copy.28), kind=kCustom, calls=%fused_computation.3 | custom fusion | flops 2097152 | bytes 25166336 | tf_op jit(solution)/shard_map/scatter-add | solution.py:34
  74.5 4.9 fusion.2
  79.4 0.0 all-to-all-done
  79.4 9.9 %all-to-all-start.1 = ((bf16[32,256,128]{2,1,0:T(8,128)(2,1)}), bf16[32,256,128]{2,1,0:T(8,128)(2,1)}, u32[]{:S(2)}, u32[]{:S(2)}) async-start(bf16[32,256,128]{2,1,0:T(8,128)(2,1)} %fusion.2), calls=%async_computation.1 | async-start | bytes 4194304 | tf_op jit(solution)/shard_map/all_to_all | solution.py:42
  89.3 0.0 reduce-scatter.2.cloned.1.call-start
  89.4 5.5 fusion.31
  94.8 0.1 compare_select_fusion.2
  94.9 44.0 %all-to-all-done.1 = bf16[32,256,128]{2,1,0:T(8,128)(2,1)} async-done(((bf16[32,256,128]{2,1,0:T(8,128)(2,1)}), bf16[32,256,128]{2,1,0:T(8,128)(2,1)}, u32[]{:S(2)}, u32[]{:S(2)}) %all-to-all-start.1) | async-done | bytes 2097184 | tf_op jit(solution)/shard_map/all_to_all | solution.py:42
  138.9 45.6 %scatter_custom_fusion.1 = f32[2048,128]{1,0:T(8,128)} fusion(s32[8192]{0:T(1024)S(1)} %bitcast.74, bf16[8192,128]{1,0:T(8,128)(2,1)} %bitcast.18, f32[]{:T(128)} %constant.32.clone.1), kind=kCustom, calls=%fused_computation.7 | custom fusion | flops 2097152 | bytes 3145732 | tf_op jit(solution)/shard_map/scatter-add | solution.py:50
  184.4 8.3 %convolution_add_fusion = f32[1024,2048]{1,0:T(8,128)} fusion(f32[1024,2048]{1,0:T(8,128)} %fusion.31, bf16[1024,1024]{1,0:T(8,128)(2,1)S(1)} %copy-done, s32[]{:T(128)S(6)} %select_n.95, f32[2048,128]{1,0:T(8,128)} %scatter_custom_fusion.1, f32[2048]{0:T(1024)S(1)} %convert_element_type.35), kind=kOutput, calls=%fused_computation.6 | convolution fusion | flops 539492352 | bytes 18096132 | tf_op jit(solution)/shard_map/dot_general | solution.py:59
  192.8 0.0 reduce-scatter.2.cloned.1.call-update
  192.8 1.2 copy.29
  194.0 48.9 %reduce-scatter.2.cloned.1.call-done = f32[128,2048]{1,0:T(8,128)} async-done(((f32[1024,2048]{1,0:T(8,128)}), f32[128,2048]{1,0:T(8,128)}) %reduce-scatter.2.cloned.1.call-update) | async-done | bytes 1048592 | tf_op jit(solution)/shard_map/reduce_scatter | solution.py:62
  242.9 2.5 fusion.26
  245.4 2.5 stack.2
  247.9 7.4 %all-to-all-start.2 = ((bf16[8,2048,128]{1,2,0:T(8,128)(2,1)}), bf16[8,2048,128]{1,2,0:T(8,128)(2,1)}, u32[]{:S(2)}, u32[]{:S(2)}) async-start(bf16[8,2048,128]{1,2,0:T(8,128)(2,1)} %stack.2), calls=%async_computation.3 | async-start | bytes 8388608 | tf_op jit(solution)/shard_map/all_to_all | solution.py:66
  255.3 0.1 compare_select_fusion
  255.3 48.2 %all-to-all-done.2 = bf16[8,2048,128]{1,2,0:T(8,128)(2,1)} async-done(((bf16[8,2048,128]{1,2,0:T(8,128)(2,1)}), bf16[8,2048,128]{1,2,0:T(8,128)(2,1)}, u32[]{:S(2)}, u32[]{:S(2)}) %all-to-all-start.2) | async-done | bytes 4194336 | tf_op jit(solution)/shard_map/all_to_all | solution.py:66
  303.6 3.6 fusion.16
  307.2 24.0 %gather_fusion.1 = bf16[8192,128]{1,0:T(8,128)(2,1)S(1)} fusion(bf16[2048,128]{1,0:T(8,128)(2,1)S(1)} %fusion.16, s32[8192]{0:T(1024)S(1)} %broadcast_clamp_fusion), kind=kCustom, calls=%fused_computation.1 | custom fusion | bytes 4227072 | tf_op jit(solution)/shard_map/jit(_take)/gather | solution.py:88
  331.3 4.6 select_select_fusion
  335.9 9.9 %all-to-all-start.3 = ((bf16[32,256,128]{2,1,0:T(8,128)(2,1)}), bf16[32,256,128]{2,1,0:T(8,128)(2,1)S(1)}, u32[]{:S(2)}, u32[]{:S(2)}) async-start(bf16[32,256,128]{2,1,0:T(8,128)(2,1)} %select_select_fusion), calls=%async_computation.4 | async-start | bytes 4194304 | tf_op jit(solution)/shard_map/all_to_all | solution.py:89
  345.8 0.0 all-reduce.3.cloned.1.call-start
  345.8 4.3 convolution_bitcast_fusion
  350.1 5.1 fusion.39
  355.2 0.0 all-reduce.3.cloned.1.call-update
  355.3 1.0 copy.32
  356.3 159.5 %all-reduce.3.cloned.1.call-done = (f32[128,1024]{0,1:T(8,128)}, f32[128,1024]{1,0:T(8,128)}) async-done(((f32[128,1024]{0,1:T(8,128)}, f32[128,1024]{1,0:T(8,128)}), (f32[128,1024]{0,1:T(8,128)}, f32[128,1024]{1,0:T(8,128)})) %all-reduce.3.cloned.1.call-update) | async-done | bytes 1048592 | tf_op jit(solution)/shard_map/psum | solution.py:77
  515.8 2.0 copy.33
  517.8 0.0 all-to-all-done.3
  517.8 3.0 gather_fusion.2
  520.8 8.4 %fusion.12 = f32[128,128,128]{1,2,0:T(8,128)} fusion(bf16[128,128,128]{2,1,0:T(8,128)(2,1)} %param.13, bf16[128,128,128]{2,1,0:T(8,128)(2,1)} %gather_fusion.2, pred[128]{0:T(512)(128)(4,1)S(1)} %compare_and_fusion.1), kind=kOutput, calls=%fused_computation.18 | convolution fusion | flops 538968064 | bytes 16777344 | tf_op jit(solution)/shard_map/kij,kid->kjd/dot_general | solution.py:92
  529.2 9.0 %copy.31 = f32[128,128,128]{2,1,0:T(8,128)} copy(f32[128,128,128]{1,2,0:T(8,128)} %fusion.12) | data formatting | bytes 16777216 | tf_op jit(solution)/shard_map/kij,kid->kjd/dot_general | solution.py:92
  538.2 0.1 broadcast_in_dim.98
  538.3 17.0 %scatter_fusion.1 = f32[16,128,128]{2,1,0:T(8,128)S(1)} fusion(f32[16,128,128]{2,1,0:T(8,128)S(1)} %broadcast_in_dim.98, s32[128]{0:T(128)S(1)} %copy-done.8, f32[128,128,128]{2,1,0:T(8,128)} %copy.31), kind=kCustom, calls=%fused_computation.5 | custom fusion | flops 2097152 | bytes 25166336 | tf_op jit(solution)/shard_map/scatter-add | solution.py:93
  555.4 0.0 copy-start.1
  555.4 4.5 fusion.15
  559.8 0.8 copy.45
  (23 shorter events, 0.1 us)
Async XLA Ops:
  7.2 177.3 %copy-start = (bf16[1024,1024]{1,0:T(8,128)(2,1)S(1)}, bf16[1024,1024]{1,0:T(8,128)(2,1)}, u32[]{:S(2)}) copy-start(bf16[1024,1024]{1,0:T(8,128)(2,1)} %param.12) | copy-start | bytes 6291460
  8.8 70.6 %all-to-all-start = ((s32[32,1,256]{2,1,0:T(1,128)}), s32[32,1,256]{2,1,0:T(1,128)S(1)}, u32[]{:S(2)}, u32[]{:S(2)}) async-start(s32[32,1,256]{2,1,0:T(1,128)} %compare_select_fusion.4), calls=%async_computation | async-start | bytes 65536 | tf_op jit(solution)/shard_map/all_to_all | solution.py:43
  45.4 2.5 copy-start.7
  74.5 14.8 %copy-start.6 = (s32[2048]{0:T(1024)S(1)}, s32[2048]{0:T(1024)}, u32[]{:S(2)}) copy-start(s32[2048]{0:T(1024)} %param.18) | copy-start | bytes 24580
  74.5 14.8 %copy-start.2 = (bf16[2048,128]{1,0:T(8,128)(2,1)S(1)}, bf16[2048,128]{1,0:T(8,128)(2,1)}, u32[]{:S(2)}) copy-start(bf16[2048,128]{1,0:T(8,128)(2,1)} %param.10) | copy-start | bytes 1572868
  79.4 59.5 %all-to-all-start.1 = ((bf16[32,256,128]{2,1,0:T(8,128)(2,1)}), bf16[32,256,128]{2,1,0:T(8,128)(2,1)}, u32[]{:S(2)}, u32[]{:S(2)}) async-start(bf16[32,256,128]{2,1,0:T(8,128)(2,1)} %fusion.2), calls=%async_computation.1 | async-start | bytes 4194304 | tf_op jit(solution)/shard_map/all_to_all | solution.py:42
  89.3 153.6 %reduce-scatter.2.cloned.1.call-start = ((), (), s32[]{:S(2)}) async-start(), calls=%async_computation.5 | async-start | bytes 9437184 | tf_op jit(solution)/shard_map/reduce_scatter | solution.py:62
  247.9 55.7 %all-to-all-start.2 = ((bf16[8,2048,128]{1,2,0:T(8,128)(2,1)}), bf16[8,2048,128]{1,2,0:T(8,128)(2,1)}, u32[]{:S(2)}, u32[]{:S(2)}) async-start(bf16[8,2048,128]{1,2,0:T(8,128)(2,1)} %stack.2), calls=%async_computation.3 | async-start | bytes 8388608 | tf_op jit(solution)/shard_map/all_to_all | solution.py:66
  335.9 181.9 %all-to-all-start.3 = ((bf16[32,256,128]{2,1,0:T(8,128)(2,1)}), bf16[32,256,128]{2,1,0:T(8,128)(2,1)S(1)}, u32[]{:S(2)}, u32[]{:S(2)}) async-start(bf16[32,256,128]{2,1,0:T(8,128)(2,1)} %select_select_fusion), calls=%async_computation.4 | async-start | bytes 4194304 | tf_op jit(solution)/shard_map/all_to_all | solution.py:89
  345.8 170.0 %all-reduce.3.cloned.1.call-start = ((), (), s32[]{:S(2)}) async-start(), calls=%async_computation.6 | async-start | bytes 2097152 | tf_op jit(solution)/shard_map/psum | solution.py:77
  345.8 4.3 copy-start.3
  350.1 5.1 copy-start.4
  529.2 9.1 %copy-start.8 = (s32[128]{0:T(128)S(1)}, s32[128]{0:T(128)}, u32[]{:S(2)}) copy-start(s32[128]{0:T(128)} %param.14) | copy-start | bytes 1540
  555.3 4.5 copy-start.5
  555.4 5.3 copy-start.1
Sparse Core Ops, SparseCore 0:
  192.9 49.9 reduce-scatter.1
  355.3 160.3 all-reduce.2
